TPU v7x, 128 devices: a whole 4x4x4 slice. The times are simulated.
128 devices in a mesh: row: 16 (over y, x), col: 8 (over z, core).
Axes of the slice: x: 4, y: 4, z: 4, core: 2. Of those that a mesh axis runs over, the one named last changes fastest.
Arguments:
- orbitals: float32 [32768, 1024], P('row', 'col'), may hold values from -6 to 6
- point_index: int32 [8192], replicated, may hold values from 0 to 32767, as said below
- coulomb: float32 [8192, 8192], P('row', 'col'), may hold values from -0.001953125 to 0.001953125
- fitting: float32 [32768, 8192], P('row', 'col'), may hold values from -0.0625 to 0.0625
Outputs:
- exchange_out: float32 [32768, 1024], P('row', 'col')
Inputs may be any that keep to these rules, and one draw needn't show every extreme that they name: `point_index`: indices are distinct. Grid index g lies in slab g // 2048. Of the 512 consecutive points of each row panel, at most 64 lie in one slab, and in every panel exactly 64 lie in one slab.
All inputs are finite; a program needn't handle non-finite values.
Results may differ from a plain program's by a relative error of at most 0.00012.
Values sent between devices are 32-bit elements; how exact they have to be, the bound alone decides.
No kernel may reach another device: no remote copies, remote signals or barrier semaphores. Data moves between devices by JAX's collectives and lax.ppermute only.
A program may use at most 64 MiB of HBM per device.

v0:
```python
import jax
import jax.numpy as jnp
from jax import lax
from jax.sharding import PartitionSpec as P


def per_device(orbitals, point_index, coulomb, fitting):
    row_count = lax.axis_size("row")
    slab_rows = orbitals.shape[0]
    band_cols = orbitals.shape[1]
    total_points = point_index.shape[0]
    per_panel = total_points // row_count
    slot_count = 2 * per_panel // row_count
    my_row = lax.axis_index("row")
    my_col = lax.axis_index("col")
    owner = point_index // slab_rows
    local_row = point_index - owner * slab_rows
    owner_grid = owner.reshape(row_count, per_panel)
    local_grid = local_row.reshape(row_count, per_panel)
    matches = (owner_grid[:, :, None] == jnp.arange(row_count)[None, None, :]).astype(jnp.int32)
    ranking = jnp.cumsum(matches, axis=1) - 1
    slot_grid = jnp.sum(jnp.where(matches > 0, ranking, 0), axis=2)
    mine = owner_grid == my_row
    chosen = mine[:, :, None] & (slot_grid[:, :, None] == jnp.arange(slot_count)[None, None, :])
    source_row = jnp.sum(jnp.where(chosen, local_grid[:, :, None], 0), axis=1)
    valid = jnp.any(chosen, axis=1)
    outgoing = jnp.where(valid[:, :, None], orbitals[source_row], 0.0)
    received = lax.all_to_all(outgoing, "row", split_axis=0, concat_axis=0, tiled=True)
    flattened = received.reshape(row_count * slot_count, band_cols)
    owner_mine = lax.dynamic_slice_in_dim(owner_grid, my_row, 1, 0)[0]
    slot_mine = lax.dynamic_slice_in_dim(slot_grid, my_row, 1, 0)[0]
    panel_strip = flattened[owner_mine * slot_count + slot_mine]
    panel_full = lax.all_gather(panel_strip, "col", axis=1, tiled=True)
    strip_all = lax.all_gather(panel_strip, "row", axis=0, tiled=True)
    column_full = lax.all_to_all(strip_all, "col", split_axis=0, concat_axis=1, tiled=True)
    pair = jnp.dot(
        panel_full,
        column_full.T,
        precision=lax.Precision.HIGHEST,
        preferred_element_type=jnp.float32,
    )
    partial_value = jnp.dot(
        coulomb * pair,
        column_full,
        precision=lax.Precision.HIGHEST,
        preferred_element_type=jnp.float32,
    )
    summed = lax.psum(partial_value, "col")
    weight_strip = lax.dynamic_slice_in_dim(summed, my_col * band_cols, band_cols, 1)
    weight_all = lax.all_gather(weight_strip, "row", axis=0, tiled=True)
    weight_column = lax.all_to_all(weight_all, "col", split_axis=0, concat_axis=1, tiled=True)
    term = -jnp.dot(
        fitting, weight_column, precision=lax.Precision.HIGHEST, preferred_element_type=jnp.float32
    )
    return lax.psum_scatter(term, "col", scatter_dimension=1, tiled=True)


def solution(mesh):
    in_specs = (P("row", "col"), P(), P("row", "col"), P("row", "col"))
    out_specs = P("row", "col")
    return jax.shard_map(
        per_device, mesh=mesh, in_specs=in_specs, out_specs=out_specs, check_vma=False
    )
```

profile of v0, /device:TPU:1, one launch (start us, length us, event | category | flops | bytes accessed | tf_op | source)
XLA Modules:
  0.0 455.0 jit_solution(17053227646644260959)
XLA Ops:
  6.5 0.9 add_select_fusion
  7.4 0.1 fusion.6
  7.5 18.1 %reduce-window.6 = s32[16,16,4,128]{3,1,2,0:T(8,128)S(1)} reduce-window(s32[16,16,4,128]{3,1,2,0:T(8,128)S(1)} %fusion.6, s32[]{:T(128)} %constant.16.clone.1), window={size=1x1x1x128 pad=0_0x0_0x0_0x127_0}, to_apply=%region_0.1 | reduce-window | flops 16646144 | bytes 1048580 | tf_op jit(solution)/shard_map/reduce-window
  25.6 0.2 slice.12
  25.9 0.4 copy.12
  26.3 0.1 fusion.8
  26.5 0.2 fusion.5
  26.7 0.4 fusion.3
  27.1 0.5 select_reduce_fusion
  27.7 0.1 reshape.84
  27.7 2.8 gather_fusion
  30.6 1.0 broadcast_select_fusion
  31.6 7.6 %all-to-all-start = ((f32[16,64,128]{2,1,0:T(8,128)}), f32[16,64,128]{2,1,0:T(8,128)S(1)}, u32[]{:S(2)}, u32[]{:S(2)}) async-start(f32[16,64,128]{2,1,0:T(8,128)} %broadcast_select_fusion), calls=%async_computation | async-start | bytes 1048576 | tf_op jit(solution)/shard_map/all_to_all | solution.py:28
  39.2 10.3 %all-to-all-done = f32[16,64,128]{2,1,0:T(8,128)S(1)} async-done(((f32[16,64,128]{2,1,0:T(8,128)}), f32[16,64,128]{2,1,0:T(8,128)S(1)}, u32[]{:S(2)}, u32[]{:S(2)}) %all-to-all-start) | async-done | bytes 524320 | tf_op jit(solution)/shard_map/all_to_all | solution.py:28
  49.6 1.6 gather_fusion.1
  51.3 0.7 all-gather.8.cloned.1.call-update
  52.0 50.4 %all-gather.10.cloned.1.call-done = f32[8192,128]{1,0:T(8,128)} async-done(((f32[512,128]{1,0:T(8,128)}), f32[8192,128]{1,0:T(8,128)}) %all-gather.10.cloned.1.call-update) | async-done | bytes 4194320 | tf_op jit(solution)/shard_map/all_gather | solution.py:34
  102.4 5.4 %copy.15 = f32[8,1024,128]{1,2,0:T(8,128)} copy(f32[8,1024,128]{2,1,0:T(8,128)} %bitcast.44) | data formatting | bytes 8388608 | tf_op jit(solution)/shard_map/all_to_all | solution.py:35
  107.7 5.3 %all-to-all-start.1 = ((f32[8,1024,128]{1,2,0:T(8,128)}), f32[8,1024,128]{1,2,0:T(8,128)}, u32[]{:S(2)}, u32[]{:S(2)}) async-start(f32[8,1024,128]{1,2,0:T(8,128)} %copy.15), calls=%async_computation.1 | async-start | bytes 8388608 | tf_op jit(solution)/shard_map/all_to_all | solution.py:35
  113.0 31.5 %all-gather.8.cloned.1.call-done = f32[512,1024]{1,0:T(8,128)} async-done(((f32[512,128]{1,0:T(8,128)}), f32[512,1024]{1,0:T(8,128)}) %all-gather.8.cloned.1.call-update) | async-done | bytes 2097168 | tf_op jit(solution)/shard_map/all_gather | solution.py:33
  144.5 25.7 %all-to-all-done.1 = f32[8,1024,128]{1,2,0:T(8,128)} async-done(((f32[8,1024,128]{1,2,0:T(8,128)}), f32[8,1024,128]{1,2,0:T(8,128)}, u32[]{:S(2)}, u32[]{:S(2)}) %all-to-all-start.1) | async-done | bytes 4194336 | tf_op jit(solution)/shard_map/all_to_all | solution.py:35
  170.2 9.8 %fusion.11 = f32[512,1024]{1,0:T(8,128)S(1)} fusion(f32[512,1024]{1,0:T(8,128)} %all-gather.8.cloned.1.call-done, f32[1024,1024]{0,1:T(8,128)} %bitcast.10), kind=kOutput, calls=%fused_computation.34 | convolution fusion | flops 6442450944 | bytes 8388608 | tf_op jit(solution)/shard_map/dot_general | solution.py:36
  180.0 9.8 %fusion = f32[512,1024]{1,0:T(8,128)} fusion(f32[1024,1024]{0,1:T(8,128)} %bitcast.10, f32[512,1024]{1,0:T(8,128)S(1)} %copy-done.1, f32[512,1024]{1,0:T(8,128)S(1)} %fusion.11), kind=kOutput, calls=%fused_computation.3 | convolution fusion | flops 6442975232 | bytes 10485760 | tf_op jit(solution)/shard_map/dot_general | solution.py:42
  189.8 0.0 all-gather.6.cloned.1.call-start
  189.9 62.2 %all-reduce.2.cloned.1.call-done = f32[512,1024]{1,0:T(8,128)} async-done(((f32[512,1024]{1,0:T(8,128)}), f32[512,1024]{1,0:T(8,128)}) %all-reduce.2.cloned.1.call-update) | async-done | bytes 2097168 | tf_op jit(solution)/shard_map/psum | solution.py:48
  252.1 1.7 constant_dynamic-slice_fusion
  253.8 52.7 %all-gather.6.cloned.1.call-done = f32[8192,128]{1,0:T(8,128)} async-done(((f32[512,128]{1,0:T(8,128)}), f32[8192,128]{1,0:T(8,128)}) %all-gather.6.cloned.1.call-update) | async-done | bytes 4194320 | tf_op jit(solution)/shard_map/all_gather | solution.py:50
  306.5 5.4 %copy.16 = f32[8,1024,128]{1,2,0:T(8,128)} copy(f32[8,1024,128]{2,1,0:T(8,128)} %bitcast.45) | data formatting | bytes 8388608 | tf_op jit(solution)/shard_map/all_to_all | solution.py:51
  311.9 53.9 %all_to_all.43 = f32[8,1024,128]{1,2,0:T(8,128)S(1)} all-to-all(f32[8,1024,128]{1,2,0:T(8,128)} %copy.16), channel_id=1, replica_groups=mesh['row'=16,'col'=8] {'col'}, dimensions={0} | all-to-all | bytes 8388608 | tf_op jit(solution)/shard_map/all_to_all | solution.py:51
  365.8 29.9 %negate_bitcast_fusion = f32[2048,1024]{0,1:T(8,128)} fusion(f32[1024,1024]{0,1:T(8,128)S(1)} %bitcast.46, f32[2048,1024]{1,0:T(8,128)} %param.7), kind=kOutput, calls=%fused_computation.2 | convolution fusion | flops 25771900928 | bytes 20971520 | tf_op jit(solution)/shard_map/dot_general | solution.py:52
  395.7 50.2 %reduce-scatter.2.cloned.1.call-done = f32[2048,128]{0,1:T(8,128)} async-done(((f32[2048,1024]{0,1:T(8,128)}), f32[2048,128]{0,1:T(8,128)}) %reduce-scatter.2.cloned.1.call-update) | async-done | bytes 1048592 | tf_op jit(solution)/shard_map/reduce_scatter | solution.py:55
  445.9 2.5 copy.17
  (21 shorter events, 0.3 us)
Async XLA Ops:
  6.5 21.2 %copy-start = (f32[2048,128]{1,0:T(8,128)S(1)}, f32[2048,128]{1,0:T(8,128)}, u32[]{:S(2)}) copy-start(f32[2048,128]{1,0:T(8,128)} %param.4) | copy-start | bytes 3145732
  31.6 18.0 %all-to-all-start = ((f32[16,64,128]{2,1,0:T(8,128)}), f32[16,64,128]{2,1,0:T(8,128)S(1)}, u32[]{:S(2)}, u32[]{:S(2)}) async-start(f32[16,64,128]{2,1,0:T(8,128)} %broadcast_select_fusion), calls=%async_computation | async-start | bytes 1048576 | tf_op jit(solution)/shard_map/all_to_all | solution.py:28
  39.1 63.2 %all-gather.10.cloned.1.call-start = ((), (), s32[]{:S(2)}) async-start(), calls=%async_computation.8 | async-start | bytes 4456448 | tf_op jit(solution)/shard_map/all_gather | solution.py:34
  51.2 93.3 %all-gather.8.cloned.1.call-start = ((), (), s32[]{:S(2)}) async-start(), calls=%async_computation.7 | async-start | bytes 2359296 | tf_op jit(solution)/shard_map/all_gather | solution.py:33
  107.7 62.5 %all-to-all-start.1 = ((f32[8,1024,128]{1,2,0:T(8,128)}), f32[8,1024,128]{1,2,0:T(8,128)}, u32[]{:S(2)}, u32[]{:S(2)}) async-start(f32[8,1024,128]{1,2,0:T(8,128)} %copy.15), calls=%async_computation.1 | async-start | bytes 8388608 | tf_op jit(solution)/shard_map/all_to_all | solution.py:35
  113.0 139.1 %all-reduce.2.cloned.1.call-start = ((), (), s32[]{:S(2)}) async-start(), calls=%async_computation.4 | async-start | bytes 4194304 | tf_op jit(solution)/shard_map/psum | solution.py:48
  170.2 9.8 %copy-start.1 = (f32[512,1024]{1,0:T(8,128)S(1)}, f32[512,1024]{1,0:T(8,128)}, u32[]{:S(2)}) copy-start(f32[512,1024]{1,0:T(8,128)} %param.6) | copy-start | bytes 6291460
  189.8 116.7 %all-gather.6.cloned.1.call-start = ((), (), s32[]{:S(2)}) async-start(), calls=%async_computation.5 | async-start | bytes 4456448 | tf_op jit(solution)/shard_map/all_gather | solution.py:50
  253.7 192.2 %reduce-scatter.2.cloned.1.call-start = ((), (), s32[]{:S(2)}) async-start(), calls=%async_computation.6 | async-start | bytes 9437184 | tf_op jit(solution)/shard_map/reduce_scatter | solution.py:55
Sparse Core Ops, SparseCore 0:
  51.3 50.9 all-gather.9
  104.0 40.3 all-gather.7
  190.0 62.0 all-reduce.1
  254.1 52.4 all-gather.5
  395.8 50.0 reduce-scatter.1
where the time goes:
time: 456 us; the launch traced here: 455 us
  waiting for transfers between devices  284 us (62%)
  blocking collectives  53.9 us (12%)
  matrix products  49.4 us (11%)
  other arithmetic  21.4 us (5%)
  local copies, waits for them, and re-layouts  20.1 us (4%)
  between operations  13.3 us (3%)
  starting transfers between devices  13 us (3%)
    psum x1, waiting for transfers between devices, per_device(): summed = lax.psum(partial_value, 'col')  62.2 us
    all_to_all x1, blocking collectives, per_device(): lax.all_to_all(weight_all, 'col', split_axis=0, concat_axis=1, tiled=True)  53.9 us
    all_gather x1, waiting for transfers between devices, per_device(): weight_all = lax.all_gather(weight_strip, 'row', axis=0, tiled=True)  52.7 us
    all_gather x1, waiting for transfers between devices, per_device(): strip_all = lax.all_gather(panel_strip, 'row', axis=0, tiled=True)  50.4 us
    reduce_scatter x1, waiting for transfers between devices, per_device(): return lax.psum_scatter(term, 'col', scatter_dimension=1, tiled=True)  50.2 us
    all_gather x1, waiting for transfers between devices, per_device(): panel_full = lax.all_gather(panel_strip, 'col', axis=1, tiled=True)  31.5 us
    dot_general x1, matrix products, per_device(): jnp.dot(fitting, weight_column, precision=lax.Precision.HIGHEST, preferre...  29.9 us
    all_to_all x1, waiting for transfers between devices, per_device(): lax.all_to_all(strip_all, 'col', split_axis=0, concat_axis=1, tiled=True)  25.7 us
  transfers between devices with their start and end apart: 7, of which 7 were waited for; matrix products, arithmetic and copies ran while one was open for 1% of the time, Pallas kernels for 0%

commit v1 on v0

--- a/solution.py
+++ b/solution.py
@@ -31,7 +31,8 @@
     slot_mine = lax.dynamic_slice_in_dim(slot_grid, my_row, 1, 0)[0]
     panel_strip = flattened[owner_mine * slot_count + slot_mine]
     panel_full = lax.all_gather(panel_strip, "col", axis=1, tiled=True)
-    strip_all = lax.all_gather(panel_strip, "row", axis=0, tiled=True)
+    stack = jnp.stack([panel_strip] * lax.axis_size("row"))
+    strip_all = jnp.concatenate(lax.all_to_all(stack, "row", 0, 0), axis=0)
     column_full = lax.all_to_all(strip_all, "col", split_axis=0, concat_axis=1, tiled=True)
     pair = jnp.dot(
         panel_full,

time: 456 us -> 457 us (level)
  waiting for transfers between devices: 284 us -> 230 us
  blocking collectives: 53.9 us -> 107 us
    all_to_all x0 -> x1, blocking collectives: none -> 53.2 us  [per_device(): strip_all = jnp.concatenate(lax.all_to_all(stack, 'row', 0, 0), axis=0)]
    all_gather x1 -> x0, waiting for transfers between devices: 50.4 us -> none  [per_device(): strip_all = lax.all_gather(panel_strip, 'row', axis=0, tiled=True)]
    all_gather x1, waiting for transfers between devices: 31.5 us -> 0.01 us  [per_device(): panel_full = lax.all_gather(panel_strip, 'col', axis=1, tiled=True)]
    all_to_all x1, waiting for transfers between devices: 25.7 us -> 56.3 us  [per_device(): lax.all_to_all(strip_all, 'col', split_axis=0, concat_axis=1, tiled=True)]
  transfers between devices with their start and end apart: 7 -> 6, of which waited for: 7 -> 5; matrix products, arithmetic and copies ran while one was open for 1% -> 1% of each run, Pallas kernels for 0% -> 0%
where the time goes in v1:
time: 457 us; the launch traced here: 456 us
  waiting for transfers between devices  230 us (50%)
  blocking collectives  107 us (23%)
  matrix products  47.9 us (10%)
  other arithmetic  21.4 us (5%)
  local copies, waits for them, and re-layouts  20.2 us (4%)
  starting transfers between devices  15.9 us (3%)
  between operations  13.3 us (3%)
    psum x1, waiting for transfers between devices, per_device(): summed = lax.psum(partial_value, 'col')  59.7 us
    all_to_all x1, waiting for transfers between devices, per_device(): lax.all_to_all(strip_all, 'col', split_axis=0, concat_axis=1, tiled=True)  56.3 us
    all_to_all x1, blocking collectives, per_device(): lax.all_to_all(weight_all, 'col', split_axis=0, concat_axis=1, tiled=True)  53.9 us
    all_to_all x1, blocking collectives, per_device(): strip_all = jnp.concatenate(lax.all_to_all(stack, 'row', 0, 0), axis=0)  53.2 us
    all_gather x1, waiting for transfers between devices, per_device(): weight_all = lax.all_gather(weight_strip, 'row', axis=0, tiled=True)  52.9 us
    reduce_scatter x1, waiting for transfers between devices, per_device(): return lax.psum_scatter(term, 'col', scatter_dimension=1, tiled=True)  50.2 us
    dot_general x1, matrix products, per_device(): jnp.dot(fitting, weight_column, precision=lax.Precision.HIGHEST, preferre...  29.9 us
    another operation x2, other arithmetic  18.3 us
  transfers between devices with their start and end apart: 6, of which 5 were waited for; matrix products, arithmetic and copies ran while one was open for 1% of the time, Pallas kernels for 0%

profile of v1, /device:TPU:1, one launch (start us, length us, event | category | flops | bytes accessed | tf_op | source)
XLA Modules:
  0.0 456.0 jit_solution(13357987782297757439)
XLA Ops:
  6.5 0.9 add_select_fusion
  7.5 18.1 %reduce-window.6 = s32[16,16,4,128]{3,1,2,0:T(8,128)S(1)} reduce-window(s32[16,16,4,128]{3,1,2,0:T(8,128)S(1)} %fusion.6, s32[]{:T(128)} %constant.16.clone.1), window={size=1x1x1x128 pad=0_0x0_0x0_0x127_0}, to_apply=%region_0.1 | reduce-window | flops 16646144 | bytes 1048580 | tf_op jit(solution)/shard_map/reduce-window
  25.6 0.2 slice.12
  25.9 0.4 copy.17
  26.3 0.1 fusion.8
  26.5 0.2 fusion.5
  26.7 0.4 fusion.3
  27.1 0.5 select_reduce_fusion
  27.7 0.1 reshape.88
  27.7 2.8 gather_fusion
  30.6 1.0 broadcast_select_fusion
  31.6 7.6 %all-to-all-start = ((f32[16,64,128]{2,1,0:T(8,128)}), f32[16,64,128]{2,1,0:T(8,128)S(1)}, u32[]{:S(2)}, u32[]{:S(2)}) async-start(f32[16,64,128]{2,1,0:T(8,128)} %broadcast_select_fusion), calls=%async_computation | async-start | bytes 1048576 | tf_op jit(solution)/shard_map/all_to_all | solution.py:28
  39.2 10.4 %all-to-all-done = f32[16,64,128]{2,1,0:T(8,128)S(1)} async-done(((f32[16,64,128]{2,1,0:T(8,128)}), f32[16,64,128]{2,1,0:T(8,128)S(1)}, u32[]{:S(2)}, u32[]{:S(2)}) %all-to-all-start) | async-done | bytes 524320 | tf_op jit(solution)/shard_map/all_to_all | solution.py:28
  49.6 1.0 gather_fusion.1
  50.6 0.4 stack.2
  51.0 0.3 copy-done.2
  51.3 53.2 %all_to_all.48 = f32[16,512,128]{2,1,0:T(8,128)} all-to-all(f32[16,512,128]{2,1,0:T(8,128)S(1)} %stack.2), channel_id=1, replica_groups=mesh['row'=16,'col'=8] {'row'}, dimensions={0} | all-to-all | bytes 8388608 | tf_op jit(solution)/shard_map/all_to_all | solution.py:35
  104.5 8.0 %all-to-all-start.2 = ((f32[8,1024,128]{2,1,0:T(8,128)}), f32[8,1024,128]{2,1,0:T(8,128)}, u32[]{:S(2)}, u32[]{:S(2)}) async-start(f32[8,1024,128]{2,1,0:T(8,128)} %bitcast.44), calls=%async_computation.2 | async-start | bytes 8388608 | tf_op jit(solution)/shard_map/all_to_all | solution.py:36
  112.5 0.7 all-gather.6.cloned.1.call-update
  113.2 0.2 all-reduce.2.cloned.1.call-start
  113.5 56.3 %all-to-all-done.2 = f32[8,1024,128]{2,1,0:T(8,128)} async-done(((f32[8,1024,128]{2,1,0:T(8,128)}), f32[8,1024,128]{2,1,0:T(8,128)}, u32[]{:S(2)}, u32[]{:S(2)}) %all-to-all-start.2) | async-done | bytes 4194336 | tf_op jit(solution)/shard_map/all_to_all | solution.py:36
  169.7 5.4 %copy.20 = f32[1024,8,128]{0,2,1:T(8,128)} copy(f32[1024,8,128]{2,0,1:T(8,128)} %bitcast.9) | data formatting | bytes 8388608 | tf_op jit(solution)/shard_map/all_to_all | solution.py:36
  175.1 9.8 %fusion.11 = f32[512,1024]{1,0:T(8,128)S(1)} fusion(f32[512,1024]{1,0:T(8,128)} %all-gather.6.cloned.1.call-done, f32[1024,1024]{0,1:T(8,128)} %bitcast.42), kind=kOutput, calls=%fused_computation.34 | convolution fusion | flops 6442450944 | bytes 8388608 | tf_op jit(solution)/shard_map/dot_general | solution.py:37
  184.9 8.2 %fusion = f32[512,1024]{1,0:T(8,128)} fusion(f32[1024,1024]{0,1:T(8,128)S(1)} %bitcast.43, f32[512,1024]{1,0:T(8,128)S(1)} %copy-done.3, f32[512,1024]{1,0:T(8,128)S(1)} %fusion.11), kind=kOutput, calls=%fused_computation.3 | convolution fusion | flops 6442975232 | bytes 10485760 | tf_op jit(solution)/shard_map/dot_general | solution.py:43
  193.2 59.7 %all-reduce.2.cloned.1.call-done = f32[512,1024]{1,0:T(8,128)} async-done(((f32[512,1024]{1,0:T(8,128)}), f32[512,1024]{1,0:T(8,128)}) %all-reduce.2.cloned.1.call-update) | async-done | bytes 2097168 | tf_op jit(solution)/shard_map/psum | solution.py:49
  252.9 1.7 constant_dynamic-slice_fusion
  254.7 52.9 %all-gather.4.cloned.1.call-done = f32[8192,128]{1,0:T(8,128)} async-done(((f32[512,128]{1,0:T(8,128)}), f32[8192,128]{1,0:T(8,128)}) %all-gather.4.cloned.1.call-update) | async-done | bytes 4194320 | tf_op jit(solution)/shard_map/all_gather | solution.py:51
  307.6 5.4 %copy.21 = f32[8,1024,128]{1,2,0:T(8,128)} copy(f32[8,1024,128]{2,1,0:T(8,128)} %bitcast.46) | data formatting | bytes 8388608 | tf_op jit(solution)/shard_map/all_to_all | solution.py:52
  312.9 53.9 %all_to_all.49 = f32[8,1024,128]{1,2,0:T(8,128)S(1)} all-to-all(f32[8,1024,128]{1,2,0:T(8,128)} %copy.21), channel_id=1, replica_groups=mesh['row'=16,'col'=8] {'col'}, dimensions={0} | all-to-all | bytes 8388608 | tf_op jit(solution)/shard_map/all_to_all | solution.py:52
  366.8 29.9 %negate_bitcast_fusion = f32[2048,1024]{0,1:T(8,128)} fusion(f32[1024,1024]{0,1:T(8,128)S(1)} %bitcast.47, f32[2048,1024]{1,0:T(8,128)} %param.7), kind=kOutput, calls=%fused_computation.2 | convolution fusion | flops 25771900928 | bytes 20971520 | tf_op jit(solution)/shard_map/dot_general | solution.py:53
  396.7 50.2 %reduce-scatter.2.cloned.1.call-done = f32[2048,128]{0,1:T(8,128)} async-done(((f32[2048,1024]{0,1:T(8,128)}), f32[2048,128]{0,1:T(8,128)}) %reduce-scatter.2.cloned.1.call-update) | async-done | bytes 1048592 | tf_op jit(solution)/shard_map/reduce_scatter | solution.py:56
  446.9 2.5 copy.22
  (24 shorter events, 0.3 us)
Async XLA Ops:
  6.5 21.2 %copy-start = (f32[2048,128]{1,0:T(8,128)S(1)}, f32[2048,128]{1,0:T(8,128)}, u32[]{:S(2)}) copy-start(f32[2048,128]{1,0:T(8,128)} %param.4) | copy-start | bytes 3145732
  31.6 18.0 %all-to-all-start = ((f32[16,64,128]{2,1,0:T(8,128)}), f32[16,64,128]{2,1,0:T(8,128)S(1)}, u32[]{:S(2)}, u32[]{:S(2)}) async-start(f32[16,64,128]{2,1,0:T(8,128)} %broadcast_select_fusion), calls=%async_computation | async-start | bytes 1048576 | tf_op jit(solution)/shard_map/all_to_all | solution.py:28
  50.6 0.7 copy-start.2
  104.5 65.2 %all-to-all-start.2 = ((f32[8,1024,128]{2,1,0:T(8,128)}), f32[8,1024,128]{2,1,0:T(8,128)}, u32[]{:S(2)}, u32[]{:S(2)}) async-start(f32[8,1024,128]{2,1,0:T(8,128)} %bitcast.44), calls=%async_computation.2 | async-start | bytes 8388608 | tf_op jit(solution)/shard_map/all_to_all | solution.py:36
  112.5 62.6 %all-gather.6.cloned.1.call-start = ((), (), s32[]{:S(2)}) async-start(), calls=%async_computation.8 | async-start | bytes 2359296 | tf_op jit(solution)/shard_map/all_gather | solution.py:33
  113.2 139.7 %all-reduce.2.cloned.1.call-start = ((), (), s32[]{:S(2)}) async-start(), calls=%async_computation.5 | async-start | bytes 4194304 | tf_op jit(solution)/shard_map/psum | solution.py:49
  175.1 9.8 %copy-start.1 = (f32[1024,8,128]{0,2,1:T(8,128)S(1)}, f32[1024,8,128]{0,2,1:T(8,128)}, u32[]{:S(2)}) copy-start(f32[1024,8,128]{0,2,1:T(8,128)} %copy.20) | copy-start | bytes 12582916
  175.1 9.8 %copy-start.3 = (f32[512,1024]{1,0:T(8,128)S(1)}, f32[512,1024]{1,0:T(8,128)}, u32[]{:S(2)}) copy-start(f32[512,1024]{1,0:T(8,128)} %param.6) | copy-start | bytes 6291460
  193.2 114.4 %all-gather.4.cloned.1.call-start = ((), (), s32[]{:S(2)}) async-start(), calls=%async_computation.6 | async-start | bytes 4456448 | tf_op jit(solution)/shard_map/all_gather | solution.py:51
  254.6 192.3 %reduce-scatter.2.cloned.1.call-start = ((), (), s32[]{:S(2)}) async-start(), calls=%async_computation.7 | async-start | bytes 9437184 | tf_op jit(solution)/shard_map/reduce_scatter | solution.py:56
Sparse Core Ops, SparseCore 0:
  115.0 35.2 all-gather.5
  193.3 59.5 all-reduce.1
  255.1 52.4 all-gather.3
  396.8 50.0 reduce-scatter.1
